TPU v7x, 32 devices: a whole 2x2x4 slice. The times are simulated.
32 devices in a mesh: prompt: 2 (over y), tensor: 4 (over z), ctx: 4 (over x, core).
Axes of the slice: x: 2, y: 2, z: 4, core: 2. Of those that a mesh axis runs over, the one named last changes fastest.
Arguments:
- hidden_in: bfloat16 [2048, 8192], P(('prompt', 'ctx', 'tensor')), parts along dimension 0, may hold values from -6 to 6
- norm_gain: float32 [8192], replicated, may hold values from 0.1 to 1.9
- weight_in: bfloat16 [8192, 3, 4096], P('ctx', None, 'tensor'), may hold values from -0.0625 to 0.0625
- filter_taps: float32 [256, 128], P('tensor'), may hold values from -0.6 to 0.6
- filter_decay: float32 [256], P('tensor'), may hold values from 0.003 to 0.3
- skip_gain: float32 [4096], P('tensor'), may hold values from -1 to 1
- tail_cache: bfloat16 [254, 4096], P('prompt', 'tensor'), parts along dimension 0, may hold values from -6 to 6
- output_weight: bfloat16 [4096, 8192], P(None, 'tensor'), may hold values from -0.09375 to 0.09375
Outputs:
- mixer_output: bfloat16 [2048, 8192], P(('prompt', 'ctx'), 'tensor'), parts along dimension 0
There are 2 independent parts, one for each index of `prompt`. A program takes and returns all parts, laid end to end along the dimension named above; an argument that names none is the same for every part. Nothing has to cross between parts.
All inputs are finite; a program needn't handle non-finite values.
Results may differ from a plain program's by a relative error of at most 0.0095.
Values may be sent and summed in bfloat16 or wider, within the bound.
A program may use at most 256 MiB of HBM per device.

v0:
```python
import jax
import jax.numpy as jnp
from jax import lax
from jax.sharding import PartitionSpec as P

GROUP = 16


def passed_along(value, axis, steps):
    count = lax.axis_size(axis)
    leading, last = (max(0, -steps), min(count, count - steps))
    return lax.ppermute(value, axis, [(source, source + steps) for source in range(leading, last)])


def normalize_rows(hidden_in, norm_gain):
    values = hidden_in.astype(jnp.float32)
    scaled = lax.rsqrt(jnp.mean(values * values, axis=-1, keepdims=True) + 1e-06)
    return (values * scaled * norm_gain[None, :]).astype(jnp.bfloat16)


def banded_taps(taps_full, shard_rows):
    group_count, tap_count = taps_full.shape
    width = shard_rows + tap_count - 1
    first_row = jnp.concatenate(
        [taps_full[:, ::-1], jnp.zeros((group_count, width + 1 - tap_count), jnp.float32)], axis=1
    )
    repeated = jnp.tile(first_row, (1, shard_rows))
    return repeated[:, : shard_rows * width].reshape(group_count, shard_rows, width)


def on_device(
    hidden_in, norm_gain, weight_in, filter_taps, filter_decay, skip_gain, tail_cache, output_weight
):
    gathered = lax.all_gather(hidden_in, "tensor", axis=0, tiled=True)
    normed = normalize_rows(gathered, norm_gain)
    shard_rows = normed.shape[0]
    channels = weight_in.shape[2]
    qkv = jnp.einsum(
        "td,dgc->tgc",
        normed,
        lax.all_gather(weight_in, "ctx", axis=0, tiled=True),
        preferred_element_type=jnp.float32,
    )
    query = qkv[:, 0]
    product = (qkv[:, 1] * qkv[:, 2]).astype(jnp.bfloat16)
    tail_rows = filter_taps.shape[1] - 1
    incoming = passed_along(product[shard_rows - tail_rows :], "ctx", 1)
    leading = lax.axis_index("ctx") == 0
    before = jnp.where(leading, tail_cache, incoming)
    extended = jnp.concatenate([before, product], axis=0).astype(jnp.float32)
    lags = jnp.arange(filter_taps.shape[1]).astype(jnp.float32)
    taps_full = filter_taps * jnp.exp(-filter_decay[:, None] * lags[None, :])
    band = banded_taps(taps_full, shard_rows)
    group_count = taps_full.shape[0]
    grouped = extended.reshape(extended.shape[0], group_count, GROUP)
    filtered = jnp.einsum(
        "gsj,jgi->sgi",
        band,
        grouped,
        precision=lax.Precision.HIGHEST,
        preferred_element_type=jnp.float32,
    ).reshape(shard_rows, channels)
    gated = (query * (filtered + skip_gain[None, :] * product.astype(jnp.float32))).astype(
        jnp.bfloat16
    )
    totals = jnp.dot(
        lax.all_gather(gated, "tensor", axis=1, tiled=True),
        output_weight,
        preferred_element_type=jnp.float32,
    )
    return totals.astype(jnp.bfloat16)


def solution(mesh):
    in_specs = (
        P(("prompt", "ctx", "tensor"), None),
        P(),
        P("ctx", None, "tensor"),
        P("tensor", None),
        P("tensor"),
        P("tensor"),
        P("prompt", "tensor"),
        P(None, "tensor"),
    )
    out_specs = P(("prompt", "ctx"), "tensor")
    return jax.shard_map(
        on_device, mesh=mesh, in_specs=in_specs, out_specs=out_specs, check_vma=False
    )
```

profile of v0, /device:TPU:0, one launch (start us, length us, event | category | flops | bytes accessed | tf_op | source)
XLA Modules:
  0.0 509.6 jit_solution(4066531910178312621)
XLA Ops:
  6.5 0.0 all-gather.4.cloned.1.call-start
  6.5 0.7 all-gather.4.cloned.1.call-update
  7.3 0.0 all-gather.6.cloned.1.call-start
  7.3 0.7 all-gather.6.cloned.1.call-update
  8.0 0.0 all-gather.8.cloned.1.call-start
  8.1 0.0 copy-done.4
  8.1 0.0 copy-done.1
  8.1 0.1 exponential_multiply_fusion
  8.2 0.1 rev.3
  8.3 10.3 %tile.4 = f32[64,256,384]{2,1,0:T(8,128)} broadcast(f32[64,384]{1,0:T(8,128)S(1)} %concatenate.7), dimensions={0,2} | broadcast | bytes 25264128 | tf_op jit(solution)/shard_map/tile | solution.py:27
  18.6 22.1 %copy.13 = f32[8,8,256,384]{3,1,2,0:T(8,128)S(1)} copy(f32[8,8,256,384]{3,2,1,0:T(8,128)} %bitcast.25) | data formatting | bytes 50331648
  40.7 8.6 %slice.28 = f32[64,98048]{1,0:T(8,128)} slice(f32[64,98304]{1,0:T(8,128)S(1)} %bitcast.26), slice={[0:64], [0:98048]} | slice | bytes 50200576 | tf_op jit(solution)/shard_map/slice | solution.py:28
  49.3 32.8 %reshape.33 = f32[64,256,383]{2,1,0:T(8,128)} reshape(f32[64,98048]{1,0:T(8,128)} %slice.28) | data formatting | bytes 50200576 | tf_op jit(solution)/shard_map/reshape | solution.py:28
  82.1 10.3 %all-gather.4.cloned.1.call-done = bf16[256,8192]{1,0:T(8,128)(2,1)} async-done(((bf16[64,8192]{1,0:T(8,128)(2,1)}), bf16[256,8192]{1,0:T(8,128)(2,1)}) %all-gather.4.cloned.1.call-update) | async-done | bytes 4194320 | tf_op jit(solution)/shard_map/all_gather | solution.py:34
  92.4 3.1 fusion
  95.5 294.1 %all-gather.6.cloned.1.call-done = bf16[8192,3,1024]{2,0,1:T(8,128)(2,1)} async-done(((bf16[2048,3,1024]{2,0,1:T(8,128)(2,1)}), bf16[8192,3,1024]{2,0,1:T(8,128)(2,1)}) %all-gather.6.cloned.1.call-update) | async-done | bytes 50331664 | tf_op jit(solution)/shard_map/all_gather | solution.py:41
  389.7 0.0 copy-done.3
  389.7 21.9 %fusion.4 = f32[256,3,1024]{2,0,1:T(8,128)S(1)} fusion(bf16[8192,3,1024]{2,0,1:T(8,128)(2,1)} %all-gather.6.cloned.1.call-done, bf16[256,8192]{1,0:T(8,128)(2,1)} %all-gather.4.cloned.1.call-done, f32[8192]{0:T(1024)S(1)} %copy-done.3, f32[256]{0:T(256)S(1)} %add_rsqrt_fusion), kind=kOutput, calls=%fused_computation.6 | convolution fusion | flops 12893290496 | bytes 57705472 | tf_op jit(solution)/shard_map/td,dgc->tgc/dot_general | solution.py:38
  411.6 0.1 fusion.8
  411.8 0.1 slice_bitcast_fusion.1
  411.8 2.4 collective-permute-start
  414.2 0.1 fusion.17
  414.3 0.8 collective-permute-done
  415.1 0.0 copy-done
  415.2 1.0 pad_maximum_fusion
  416.2 2.3 copy.11
  418.5 17.3 %fusion.11 = f32[64,16,256]{2,1,0:T(8,128)} fusion(bf16[383,64,16]{0,2,1:T(8,128)(2,1)} %bitcast.28, f32[64,256,383]{2,1,0:T(8,128)} %reshape.33), kind=kOutput, calls=%fused_computation.21 | convolution fusion | flops 1204813824 | bytes 26933248 | tf_op jit(solution)/shard_map/gsj,jgi->sgi/dot_general | solution.py:56
  435.8 2.5 copy.12
  438.3 2.4 fusion.10
  440.7 0.0 all-gather.8.cloned.1.call-update
  440.8 50.5 %all-gather.8.cloned.1.call-done = bf16[256,4096]{1,0:T(8,128)(2,1)} async-done(((bf16[256,1024]{1,0:T(8,128)(2,1)}), bf16[256,4096]{1,0:T(8,128)(2,1)}) %all-gather.8.cloned.1.call-update) | async-done | bytes 2097168 | tf_op jit(solution)/shard_map/all_gather | solution.py:67
  491.2 11.9 %convolution_convert_fusion = bf16[256,2048]{1,0:T(8,128)(2,1)} fusion(bf16[256,4096]{1,0:T(8,128)(2,1)} %all-gather.8.cloned.1.call-done, bf16[4096,2048]{1,0:T(8,128)(2,1)} %param.15), kind=kOutput, calls=%fused_computation.9 | convolution fusion | flops 4295491584 | bytes 19922944 | tf_op jit(solution)/shard_map/dot_general | solution.py:66
  (11 shorter events, 0.1 us)
Async XLA Ops:
  6.5 1.5 copy-start.4
  6.5 1.6 copy-start.1
  6.5 85.9 %all-gather.4.cloned.1.call-start = ((), (), s32[]{:S(2)}) async-start(), calls=%async_computation | async-start | bytes 5242880 | tf_op jit(solution)/shard_map/all_gather | solution.py:34
  7.3 382.4 %all-gather.6.cloned.1.call-start = ((), (), s32[]{:S(2)}) async-start(), calls=%async_computation.1 | async-start | bytes 62914560 | tf_op jit(solution)/shard_map/all_gather | solution.py:41
  8.0 483.2 %all-gather.8.cloned.1.call-start = ((), (), s32[]{:S(2)}) async-start(), calls=%async_computation.2 | async-start | bytes 2621440 | tf_op jit(solution)/shard_map/all_gather | solution.py:67
  49.3 340.4 %copy-start.3 = (f32[8192]{0:T(1024)S(1)}, f32[8192]{0:T(1024)}, u32[]{:S(2)}) copy-start(f32[8192]{0:T(1024)} %param.9) | copy-start | bytes 98308
  95.5 319.6 %copy-start = (bf16[127,1024]{1,0:T(8,128)(2,1)S(1)}, bf16[127,1024]{1,0:T(8,128)(2,1)}, u32[]{:S(2)}) copy-start(bf16[127,1024]{1,0:T(8,128)(2,1)} %param.14) | copy-start | bytes 780292
  411.8 3.3 collective-permute-start
  418.5 19.8 %copy-start.2 = (f32[1024]{0:T(1024)S(1)}, f32[1024]{0:T(1024)}, u32[]{:S(2)}) copy-start(f32[1024]{0:T(1024)} %param.13) | copy-start | bytes 12292
Sparse Core Ops, SparseCore 0:
  8.9 83.4 all-gather.3
  94.0 295.6 all-gather.5
  440.9 50.3 all-gather.7
where the time goes:
time: 510 us
  waiting for transfers between devices  357 us (70%)
  local copies, waits for them, and re-layouts  78.8 us (15%)
  matrix products  51.1 us (10%)
  between operations  13.2 us (3%)
  other arithmetic  6.97 us (1%)
    all_gather x1, waiting for transfers between devices, on_device(): lax.all_gather(weight_in, 'ctx', axis=0, tiled=True)  294 us
    all_gather x1, waiting for transfers between devices, on_device(): lax.all_gather(gated, 'tensor', axis=1, tiled=True)  50.5 us
    reshape x1, local copies, waits for them, and re-layouts, banded_taps(): repeated[:, :shard_rows * width].reshape(group_count, shard_rows, width)  32.8 us
    unnamed x11, local copies, waits for them, and re-layouts  22.1 us
    dot_general x1, matrix products, on_device(): jnp.einsum('td,dgc->tgc', normed, lax.all_gather(weight_in, 'ctx', axis=0...  21.9 us
    dot_general x1, matrix products, on_device(): jnp.einsum('gsj,jgi->sgi', band, grouped, precision=lax.Precision.HIGHEST...  17.3 us
    dot_general x1, matrix products, on_device(): jnp.dot(lax.all_gather(gated, 'tensor', axis=1, tiled=True), output_weigh...  11.9 us
    another operation x1, local copies, waits for them, and re-layouts, banded_taps(): repeated = jnp.tile(first_row, (1, shard_rows))  10.3 us
  transfers between devices with their start and end apart: 4, of which 4 were waited for; matrix products, arithmetic and copies ran while one was open for 15% of the time, Pallas kernels for 0%

commit v1 on v0

--- a/solution.py
+++ b/solution.py
@@ -31,7 +31,14 @@
 def on_device(
     hidden_in, norm_gain, weight_in, filter_taps, filter_decay, skip_gain, tail_cache, output_weight
 ):
-    gathered = lax.all_gather(hidden_in, "tensor", axis=0, tiled=True)
+    ring = [hidden_in]
+    for hop in range(3):
+        ring.append(lax.ppermute(ring[-1], "tensor", [(dev, (dev + 1) % 4) for dev in range(4)]))
+    gathered = jnp.roll(
+        jnp.concatenate(ring[::-1], axis=0),
+        (lax.axis_index("tensor") + 1) * ring[0].shape[0],
+        axis=0,
+    )
     normed = normalize_rows(gathered, norm_gain)
     shard_rows = normed.shape[0]
     channels = weight_in.shape[2]

time: 510 us -> 430 us (0.84)
  waiting for transfers between devices: 357 us -> 269 us
  local copies, waits for them, and re-layouts: 78.8 us -> 85.6 us
    all_gather x1, waiting for transfers between devices: 294 us -> 165 us  [on_device(): lax.all_gather(weight_in, 'ctx', axis=0, tiled=True)]
    ppermute x0 -> x3, waiting for transfers between devices: none -> 51.3 us  [on_device(): lax.ppermute(ring[-1], 'tensor', [(dev, (dev + 1) % 4) for dev in range(4)])]
    all_gather x1 -> x0, waiting for transfers between devices: 10.3 us -> none  [on_device(): gathered = lax.all_gather(hidden_in, 'tensor', axis=0, tiled=True)]
    unnamed x11 -> x22, local copies, waits for them, and re-layouts: 22.1 us -> 28.6 us
  transfers between devices with their start and end apart: 4 -> 6, of which waited for: 4 -> 5; matrix products, arithmetic and copies ran while one was open for 15% -> 18% of each run, Pallas kernels for 0% -> 0%
where the time goes in v1:
time: 430 us; the launch traced here: 429 us
  waiting for transfers between devices  269 us (63%)
  local copies, waits for them, and re-layouts  85.6 us (20%)
  matrix products  51.1 us (12%)
  between operations  13.6 us (3%)
  starting transfers between devices  5.46 us (1%)
  other arithmetic  4.78 us (1%)
    all_gather x1, waiting for transfers between devices, on_device(): lax.all_gather(weight_in, 'ctx', axis=0, tiled=True)  165 us
    ppermute x3, waiting for transfers between devices, on_device(): lax.ppermute(ring[-1], 'tensor', [(dev, (dev + 1) % 4) for dev in range(4)])  51.3 us
    all_gather x1, waiting for transfers between devices, on_device(): lax.all_gather(gated, 'tensor', axis=1, tiled=True)  50.5 us
    reshape x1, local copies, waits for them, and re-layouts, banded_taps(): repeated[:, :shard_rows * width].reshape(group_count, shard_rows, width)  33 us
    unnamed x22, local copies, waits for them, and re-layouts  28.6 us
    dot_general x1, matrix products, on_device(): jnp.einsum('td,dgc->tgc', normed, lax.all_gather(weight_in, 'ctx', axis=0...  21.9 us
    dot_general x1, matrix products, on_device(): jnp.einsum('gsj,jgi->sgi', band, grouped, precision=lax.Precision.HIGHEST...  17.3 us
    dot_general x1, matrix products, on_device(): jnp.dot(lax.all_gather(gated, 'tensor', axis=1, tiled=True), output_weigh...  11.9 us
  transfers between devices with their start and end apart: 6, of which 5 were waited for; matrix products, arithmetic and copies ran while one was open for 18% of the time, Pallas kernels for 0%

profile of v1, /device:TPU:0, one launch (start us, length us, event | category | flops | bytes accessed | tf_op | source)
XLA Modules:
  0.0 429.3 jit_solution(16403634156878345419)
XLA Ops:
  6.5 0.7 all-gather.3.cloned.1.call-update
  7.3 0.5 copy-done
  7.8 3.0 collective-permute-start
  10.8 25.2 %collective-permute-done = bf16[64,8192]{1,0:T(8,128)(2,1)S(1)} collective-permute-done((bf16[64,8192]{1,0:T(8,128)(2,1)S(1)}, bf16[64,8192]{1,0:T(8,128)(2,1)S(1)}, u32[]{:S(2)}, u32[]{:S(2)}) %collective-permute-start) | collective-permute-done | bytes 1048608 | tf_op jit(solution)/shard_map/ppermute | solution.py:36
  36.0 26.1 %collective-permute-done.1 = bf16[64,8192]{1,0:T(8,128)(2,1)S(1)} collective-permute-done((bf16[64,8192]{1,0:T(8,128)(2,1)S(1)}, bf16[64,8192]{1,0:T(8,128)(2,1)S(1)}, u32[]{:S(2)}, u32[]{:S(2)}) %collective-permute-start.1) | collective-permute-done | bytes 1048608 | tf_op jit(solution)/shard_map/ppermute | solution.py:36
  62.1 0.1 exponential_multiply_fusion
  62.2 0.1 rev.3
  62.3 10.4 %tile.4 = f32[64,256,384]{2,1,0:T(8,128)} broadcast(f32[64,384]{1,0:T(8,128)S(1)} %concatenate.14), dimensions={0,2} | broadcast | bytes 25264128 | tf_op jit(solution)/shard_map/tile | solution.py:27
  72.8 21.7 %copy.13 = f32[8,8,256,384]{3,1,2,0:T(8,128)S(1)} copy(f32[8,8,256,384]{3,2,1,0:T(8,128)} %bitcast.25) | data formatting | bytes 50331648
  94.5 8.6 %slice.28 = f32[64,98048]{1,0:T(8,128)} slice(f32[64,98304]{1,0:T(8,128)S(1)} %bitcast.26), slice={[0:64], [0:98048]} | slice | bytes 50200576 | tf_op jit(solution)/shard_map/slice | solution.py:28
  103.1 33.0 %reshape.33 = f32[64,256,383]{2,1,0:T(8,128)} reshape(f32[64,98048]{1,0:T(8,128)} %slice.28) | data formatting | bytes 50200576 | tf_op jit(solution)/shard_map/reshape | solution.py:28
  136.1 1.3 constant_dynamic-update-slice_fusion.7
  137.4 0.1 constant_dynamic-update-slice_fusion.6
  137.5 0.1 constant_dynamic-update-slice_fusion.5
  137.5 0.1 constant_dynamic-update-slice_fusion.4
  137.6 1.4 constant_dynamic-update-slice_fusion.3
  139.0 0.1 constant_dynamic-update-slice_fusion.2
  139.3 3.3 copy-done.1
  142.6 0.9 fusion
  143.5 165.3 %all-gather.3.cloned.1.call-done = bf16[8192,3,1024]{2,0,1:T(8,128)(2,1)} async-done(((bf16[2048,3,1024]{2,0,1:T(8,128)(2,1)}), bf16[8192,3,1024]{2,0,1:T(8,128)(2,1)}) %all-gather.3.cloned.1.call-update) | async-done | bytes 50331664 | tf_op jit(solution)/shard_map/all_gather | solution.py:48
  308.8 21.9 %fusion.4 = f32[256,3,1024]{2,0,1:T(8,128)S(1)} fusion(bf16[8192,3,1024]{2,0,1:T(8,128)(2,1)} %all-gather.3.cloned.1.call-done, f32[8192]{0:T(1024)S(1)} %copy-done.5, f32[256]{0:T(256)S(1)} %add_rsqrt_fusion, bf16[512,8192]{1,0:T(8,128)(2,1)} %copy-done.1, s32[]{:T(128)S(6)} %select_n.22), kind=kOutput, calls=%fused_computation.6 | convolution fusion | flops 12893290496 | bytes 57705476 | tf_op jit(solution)/shard_map/td,dgc->tgc/dot_general | solution.py:45
  330.7 0.1 fusion.9
  330.9 2.4 collective-permute-start.3
  333.3 0.1 fusion.19
  333.5 1.0 collective-permute-done.3
  334.5 1.0 pad_maximum_fusion
  335.5 2.3 copy.11
  337.8 17.3 %fusion.13 = f32[64,16,256]{2,1,0:T(8,128)} fusion(bf16[383,64,16]{0,2,1:T(8,128)(2,1)} %bitcast.28, f32[64,256,383]{2,1,0:T(8,128)} %reshape.33), kind=kOutput, calls=%fused_computation.31 | convolution fusion | flops 1204813824 | bytes 26933248 | tf_op jit(solution)/shard_map/gsj,jgi->sgi/dot_general | solution.py:63
  355.1 2.5 copy.12
  357.6 2.4 fusion.11
  360.1 50.5 %all-gather.5.cloned.1.call-done = bf16[256,4096]{1,0:T(8,128)(2,1)} async-done(((bf16[256,1024]{1,0:T(8,128)(2,1)}), bf16[256,4096]{1,0:T(8,128)(2,1)}) %all-gather.5.cloned.1.call-update) | async-done | bytes 2097168 | tf_op jit(solution)/shard_map/all_gather | solution.py:74
  410.6 11.9 %convolution_convert_fusion = bf16[256,2048]{1,0:T(8,128)(2,1)} fusion(bf16[256,4096]{1,0:T(8,128)(2,1)} %all-gather.5.cloned.1.call-done, bf16[4096,2048]{1,0:T(8,128)(2,1)} %param.15), kind=kOutput, calls=%fused_computation.10 | convolution fusion | flops 4295491584 | bytes 19922944 | tf_op jit(solution)/shard_map/dot_general | solution.py:73
  (26 shorter events, 0.3 us)
Async XLA Ops:
  6.5 1.2 copy-start
  6.5 55.6 %copy-start.6 = (f32[64]{0:T(128)S(1)}, f32[64]{0:T(128)}, u32[]{:S(2)}) copy-start(f32[64]{0:T(128)} %param.12) | copy-start | bytes 772
  6.5 55.6 %copy-start.3 = (f32[64,128]{1,0:T(8,128)S(1)}, f32[64,128]{1,0:T(8,128)}, u32[]{:S(2)}) copy-start(f32[64,128]{1,0:T(8,128)} %param.11) | copy-start | bytes 98308
  6.5 302.2 %all-gather.3.cloned.1.call-start = ((), (), s32[]{:S(2)}) async-start(), calls=%async_computation | async-start | bytes 62914560 | tf_op jit(solution)/shard_map/all_gather | solution.py:48
  7.3 403.3 %all-gather.5.cloned.1.call-start = ((), (), s32[]{:S(2)}) async-start(), calls=%async_computation.1 | async-start | bytes 2621440 | tf_op jit(solution)/shard_map/all_gather | solution.py:74
  7.8 28.2 %collective-permute-start = (bf16[64,8192]{1,0:T(8,128)(2,1)S(1)}, bf16[64,8192]{1,0:T(8,128)(2,1)S(1)}, u32[]{:S(2)}, u32[]{:S(2)}) collective-permute-start(bf16[64,8192]{1,0:T(8,128)(2,1)S(1)} %copy-done), channel_id=1, source_target_pairs={{0,4},{4,8},{8,12},{12,0},{1,5},{5,9},{9,13},{13,1},{2,6},{6,10},{... | collective-permute-start | bytes 3145736 | tf_op jit(solution)/shard_map/ppermute | solution.py:36
  36.0 26.1 %collective-permute-start.1 = (bf16[64,8192]{1,0:T(8,128)(2,1)S(1)}, bf16[64,8192]{1,0:T(8,128)(2,1)S(1)}, u32[]{:S(2)}, u32[]{:S(2)}) collective-permute-start(bf16[64,8192]{1,0:T(8,128)(2,1)S(1)} %collective-permute-done), channel_id=1, source_target_pairs={{0,4},{4,8},{8,12},{12,0},{1,5},{5,9},{9,13},{13,1},{2,6},{6,10},{... | collective-permute-start | bytes 3145736 | tf_op jit(solution)/shard_map/ppermute | solution.py:36
  62.1 74.0 %collective-permute-start.2 = (bf16[64,8192]{1,0:T(8,128)(2,1)S(1)}, bf16[64,8192]{1,0:T(8,128)(2,1)}, u32[]{:S(2)}, u32[]{:S(2)}) collective-permute-start(bf16[64,8192]{1,0:T(8,128)(2,1)S(1)} %collective-permute-done.1), channel_id=1, source_target_pairs={{0,4},{4,8},{8,12},{12,0},{1,5},{5,9},{9,13},{13,1},{2,6},{6,10},{... | collective-permute-start | bytes 3145736 | tf_op jit(solution)/shard_map/ppermute | solution.py:36
  137.4 171.3 %copy-start.5 = (f32[8192]{0:T(1024)S(1)}, f32[8192]{0:T(1024)}, u32[]{:S(2)}) copy-start(f32[8192]{0:T(1024)} %param.9) | copy-start | bytes 98308
  139.2 3.3 copy-start.1
  143.5 191.0 %copy-start.2 = (bf16[127,1024]{1,0:T(8,128)(2,1)S(1)}, bf16[127,1024]{1,0:T(8,128)(2,1)}, u32[]{:S(2)}) copy-start(bf16[127,1024]{1,0:T(8,128)(2,1)} %param.14) | copy-start | bytes 780292
  330.9 3.5 collective-permute-start.3
  337.8 19.8 %copy-start.4 = (f32[1024]{0:T(1024)S(1)}, f32[1024]{0:T(1024)}, u32[]{:S(2)}) copy-start(f32[1024]{0:T(1024)} %param.13) | copy-start | bytes 12292
Sparse Core Ops, SparseCore 0:
  8.9 299.8 all-gather.2
  360.2 50.3 all-gather.4
